TPU v7x, 512 devices: a whole 4x8x8 slice. The times are simulated.
512 devices in a mesh: rows: 64 (over x, y, core), cols: 8 (over z).
Axes of the slice: x: 4, y: 8, z: 8, core: 2. Of those that a mesh axis runs over, the one named last changes fastest.
Arguments:
- eigvecs: float32 [65536, 2048], P(('rows', 'cols')), may hold values from -6 to 6
- panels: float32 [8, 65536, 256], P('cols', 'rows'), may hold values from -0.375 to 0.375
- tfactors: float32 [2, 256, 256], replicated, may hold values from -0.03125 to 0.03125
- owners: int32 [2], replicated, may hold values from 0 to 7, as said below
Outputs:
- backvecs: float32 [65536, 2048], P('rows', 'cols')
Inputs may be any that keep to these rules, and one draw needn't show every extreme that they name: `owners`: the entries are distinct slots, among them 0 and 7.
All inputs are finite; a program needn't handle non-finite values.
Results may differ from a plain program's by a relative error of at most 0.00011.
Values sent between devices are 32-bit elements; how exact they have to be, the bound alone decides.
No kernel may reach another device: no remote copies, remote signals or barrier semaphores. Data moves between devices by JAX's collectives and lax.ppermute only.
A program may use at most 64 MiB of HBM per device.

v0:
```python
import jax
import jax.numpy as jnp
from jax import lax
from jax.sharding import PartitionSpec as P


def broadcast(x, axis, root):
    mine = lax.axis_index(axis) == root
    return lax.psum(jnp.where(mine, x, jnp.zeros_like(x)), axis)


def matmul(left, right):
    return jnp.dot(left, right, precision=lax.Precision.HIGHEST, preferred_element_type=jnp.float32)


def per_device(eigvecs, panels, tfactors, owners):
    tiles = lax.all_to_all(eigvecs, "cols", split_axis=1, concat_axis=0, tiled=True)
    count = tfactors.shape[0]
    local = panels[0]
    vectors = []
    for index in range(count):
        vectors.append(broadcast(local, "cols", owners[index]))
    factors = [jnp.triu(tfactors[index]) for index in range(count)]
    result = tiles
    for index in range(count):
        proj = lax.psum(matmul(vectors[index].T, result), "rows")
        coeff = matmul(factors[index], proj)
        result = result - matmul(vectors[index], coeff)
    return result


def solution(mesh):
    placed = (P(("rows", "cols"), None), P("cols", "rows", None), P(), P())
    return jax.shard_map(
        per_device, mesh=mesh, in_specs=placed, out_specs=P("rows", "cols"), check_vma=False
    )
```

profile of v0, /device:TPU:1, one launch (start us, length us, event | category | flops | bytes accessed | tf_op | source)
XLA Modules:
  0.0 508.5 jit_solution(2413982245606252921)
XLA Ops:
  6.5 0.0 all-reduce.9.cloned.1.call-start
  6.5 0.0 copy-start.4
  6.5 0.7 copy-done.4
  7.2 0.6 fusion.10
  9.1 2.7 select_bitcast_fusion
  11.7 0.0 copy-start.1
  11.8 0.0 all-reduce.9.cloned.1.call-update
  11.8 0.0 all-reduce.5.cloned.1.call-start
  11.8 1.1 copy-done.1
  13.0 0.1 copy.8
  13.1 45.1 %all_to_all.19 = f32[128,8,256]{2,0,1:T(8,128)S(1)} all-to-all(f32[128,8,256]{2,0,1:T(8,128)S(1)} %bitcast.31), channel_id=1, replica_groups=mesh['rows'=64,'cols'=8] {'cols'}, dimensions={1} | all-to-all | bytes 2097152 | tf_op jit(solution)/shard_map/all_to_all | solution.py:17
  58.2 58.0 %all-reduce.9.cloned.1.call-done = (f32[1024,256]{1,0:T(8,128)}, f32[1024,256]{1,0:T(8,128)}) async-done(((f32[1024,256]{1,0:T(8,128)}, f32[1024,256]{1,0:T(8,128)}), (f32[1024,256]{1,0:T(8,128)}, f32[1024,256]{1,0:T(8,128)})) %all-reduce.9.cloned.1.call-update) | async-done | bytes 2097168 | tf_op jit(solution)/shard_map/psum | solution.py:9
  116.2 0.0 copy-start.2
  116.2 3.8 fusion.11
  120.0 0.0 all-reduce.5.cloned.1.call-update
  120.0 0.0 all-reduce.7.cloned.1.call-start
  120.0 188.2 %all-reduce.5.cloned.1.call-done = f32[256,256]{1,0:T(8,128)} async-done(((f32[256,256]{1,0:T(8,128)}), f32[256,256]{1,0:T(8,128)}) %all-reduce.5.cloned.1.call-update) | async-done | bytes 262160 | tf_op jit(solution)/shard_map/psum | solution.py:26
  308.2 0.0 copy-done.2
  308.2 1.4 fusion.1
  309.6 0.0 copy-start
  309.6 2.3 convolution_subtract_fusion.1
  311.9 0.0 copy-done
  311.9 0.0 copy-start.3
  312.0 2.5 fusion.12
  314.5 0.0 all-reduce.7.cloned.1.call-update
  314.5 184.1 %all-reduce.7.cloned.1.call-done = f32[256,256]{1,0:T(8,128)} async-done(((f32[256,256]{1,0:T(8,128)}), f32[256,256]{1,0:T(8,128)}) %all-reduce.7.cloned.1.call-update) | async-done | bytes 262160 | tf_op jit(solution)/shard_map/psum | solution.py:26
  498.6 0.0 copy-done.3
  498.6 1.4 fusion
  500.0 2.0 convolution_subtract_fusion
  (1 shorter events, 0.0 us)
Async XLA Ops:
  6.5 109.6 %all-reduce.9.cloned.1.call-start = ((), (), s32[]{:S(2)}) async-start(), calls=%async_computation.3 | async-start | bytes 4194304 | tf_op jit(solution)/shard_map/psum | solution.py:9
  6.5 0.7 copy-start.4
  11.7 1.2 copy-start.1
  11.8 296.5 %all-reduce.5.cloned.1.call-start = ((), (), s32[]{:S(2)}) async-start(), calls=%async_computation.1 | async-start | bytes 524288 | tf_op jit(solution)/shard_map/psum | solution.py:26
  116.2 192.1 %copy-start.2 = (f32[2,256,256]{2,1,0:T(8,128)S(1)}, f32[2,256,256]{2,1,0:T(8,128)}, u32[]{:S(2)}) copy-start(f32[2,256,256]{2,1,0:T(8,128)} %param.6) | copy-start | bytes 1572868
  120.0 378.7 %all-reduce.7.cloned.1.call-start = ((), (), s32[]{:S(2)}) async-start(), calls=%async_computation.2 | async-start | bytes 524288 | tf_op jit(solution)/shard_map/psum | solution.py:26
  309.6 2.3 copy-start
  311.9 186.7 %copy-start.3 = (f32[2,256,256]{2,1,0:T(8,128)S(1)}, f32[2,256,256]{2,1,0:T(8,128)}, u32[]{:S(2)}) copy-start(f32[2,256,256]{2,1,0:T(8,128)} %param.6) | copy-start | bytes 1572868
Sparse Core Ops, SparseCore 0:
  11.9 104.2 all-reduce.8
  120.1 188.0 all-reduce.4
  314.6 183.9 all-reduce.6
where the time goes:
time: 509 us
  waiting for transfers between devices  430 us (84%)
  blocking collectives  45.1 us (9%)
  between operations  14.5 us (3%)
  matrix products  13.3 us (3%)
    psum x2, waiting for transfers between devices, per_device(): proj = lax.psum(matmul(vectors[index].T, result), 'rows')  372 us
    psum x1, waiting for transfers between devices, broadcast(): return lax.psum(jnp.where(mine, x, jnp.zeros_like(x)), axis)  58 us
    all_to_all x1, blocking collectives, per_device(): lax.all_to_all(eigvecs, 'cols', split_axis=1, concat_axis=0, tiled=True)  45.1 us
    dot_general x6, matrix products, matmul(): jnp.dot(left, right, precision=lax.Precision.HIGHEST, preferred_element_t...  13.3 us
  transfers between devices with their start and end apart: 3, of which 3 were waited for; matrix products, arithmetic and copies ran while one was open for 0% of the time, Pallas kernels for 0%

commit v1 on v0

--- a/solution.py
+++ b/solution.py
@@ -6,7 +6,8 @@
 
 def broadcast(x, axis, root):
     mine = lax.axis_index(axis) == root
-    return lax.psum(jnp.where(mine, x, jnp.zeros_like(x)), axis)
+    obtain_counts = lambda mat, link_axis: jnp.sum(lax.all_gather(mat, axis_name=link_axis), axis=0)
+    return obtain_counts(jnp.where(mine, x, jnp.zeros_like(x)), axis)
 
 
 def matmul(left, right):

time: 509 us -> 620 us (1.22)
  waiting for transfers between devices: 430 us -> 567 us
  blocking collectives: 45.1 us -> 0 us
  starting transfers between devices: 0.09 us -> 11 us
  other arithmetic: 2.7 us -> 10.8 us
    all_gather x0 -> x2, waiting for transfers between devices: none -> 197 us  [broadcast(): lax.all_gather(mat, axis_name=link_axis)]
    psum x1 -> x0, waiting for transfers between devices: 58 us -> none  [broadcast(): return lax.psum(jnp.where(mine, x, jnp.zeros_like(x)), axis)]
    all_to_all x1 -> x0, blocking collectives: 45.1 us -> none  [per_device(): lax.all_to_all(eigvecs, 'cols', split_axis=1, concat_axis=0, tiled=True)]
    all_to_all x0 -> x1, starting transfers between devices: none -> 10.9 us  [per_device(): lax.all_to_all(eigvecs, 'cols', split_axis=1, concat_axis=0, tiled=True)]
    reduce_sum x0 -> x2, other arithmetic: none -> 8.12 us  [broadcast(): jnp.sum(lax.all_gather(mat, axis_name=link_axis), axis=0)]
  transfers between devices with their start and end apart: 3 -> 5, of which waited for: 3 -> 4; matrix products, arithmetic and copies ran while one was open for 0% -> 2% of each run, Pallas kernels for 0% -> 0%
where the time goes in v1:
time: 620 us
  waiting for transfers between devices  567 us (91%)
  between operations  14.4 us (2%)
  matrix products  12.1 us (2%)
  starting transfers between devices  11 us (2%)
  other arithmetic  10.8 us (2%)
    psum x2, waiting for transfers between devices, per_device(): proj = lax.psum(matmul(vectors[index].T, result), 'rows')  368 us
    all_gather x2, waiting for transfers between devices, broadcast(): lax.all_gather(mat, axis_name=link_axis)  197 us
  transfers between devices with their start and end apart: 5, of which 4 were waited for; matrix products, arithmetic and copies ran while one was open for 2% of the time, Pallas kernels for 0%

profile of v1, /device:TPU:1, one launch (start us, length us, event | category | flops | bytes accessed | tf_op | source)
XLA Modules:
  0.0 619.5 jit_solution(8926246261734107966)
XLA Ops:
  6.5 0.0 all-gather.3.cloned.1.call-start
  6.5 1.3 fusion.10
  9.1 2.7 broadcast_select_fusion
  11.8 0.0 all-gather.3.cloned.1.call-update
  11.8 0.0 all-gather.5.cloned.1.call-start
  11.8 0.7 all-gather.5.cloned.1.call-update
  12.6 2.3 copy.9
  14.8 10.9 %all-to-all-start = ((f32[128,8,256]{2,0,1:T(8,128)}), f32[128,8,256]{2,0,1:T(8,128)S(1)}, u32[]{:S(2)}, u32[]{:S(2)}) async-start(f32[128,8,256]{2,0,1:T(8,128)} %bitcast.24), calls=%async_computation | async-start | bytes 2097152 | tf_op jit(solution)/shard_map/all_to_all | solution.py:18
  25.7 0.0 all-reduce.3.cloned.1.call-start
  25.8 105.8 %all-gather.3.cloned.1.call-done = f32[8,1024,256]{2,1,0:T(8,128)} async-done(((f32[1,1024,256]{2,1,0:T(8,128)}), f32[8,1024,256]{2,1,0:T(8,128)}) %all-gather.3.cloned.1.call-update) | async-done | bytes 8388624 | tf_op jit(solution)/shard_map/all_gather | solution.py:9
  131.5 4.1 reduce_sum.18
  135.6 0.0 all-to-all-done
  135.6 2.5 fusion.11
  138.1 0.0 all-reduce.3.cloned.1.call-update
  138.2 0.0 all-reduce.5.cloned.1.call-start
  138.2 91.7 %all-gather.5.cloned.1.call-done = f32[8,1024,256]{2,1,0:T(8,128)} async-done(((f32[1,1024,256]{2,1,0:T(8,128)}), f32[8,1024,256]{2,1,0:T(8,128)}) %all-gather.5.cloned.1.call-update) | async-done | bytes 8388624 | tf_op jit(solution)/shard_map/all_gather | solution.py:9
  229.9 4.1 reduce_sum.19
  233.9 184.2 %all-reduce.3.cloned.1.call-done = f32[256,256]{1,0:T(8,128)} async-done(((f32[256,256]{1,0:T(8,128)}), f32[256,256]{1,0:T(8,128)}) %all-reduce.3.cloned.1.call-update) | async-done | bytes 262160 | tf_op jit(solution)/shard_map/psum | solution.py:27
  418.1 1.4 fusion.1
  419.5 1.0 convolution_subtract_fusion.1
  420.5 0.0 copy-start
  420.6 1.0 copy-done
  421.5 2.5 fusion.12
  424.0 0.0 all-reduce.5.cloned.1.call-update
  424.1 184.3 %all-reduce.5.cloned.1.call-done = f32[256,256]{1,0:T(8,128)} async-done(((f32[256,256]{1,0:T(8,128)}), f32[256,256]{1,0:T(8,128)}) %all-reduce.5.cloned.1.call-update) | async-done | bytes 262160 | tf_op jit(solution)/shard_map/psum | solution.py:27
  608.3 1.4 fusion
  609.8 3.2 convolution_subtract_fusion
  (1 shorter events, 0.0 us)
Async XLA Ops:
  6.5 125.0 %all-gather.3.cloned.1.call-start = ((), (), s32[]{:S(2)}) async-start(), calls=%async_computation.1 | async-start | bytes 9437184 | tf_op jit(solution)/shard_map/all_gather | solution.py:9
  11.8 218.1 %all-gather.5.cloned.1.call-start = ((), (), s32[]{:S(2)}) async-start(), calls=%async_computation.3 | async-start | bytes 9437184 | tf_op jit(solution)/shard_map/all_gather | solution.py:9
  14.8 120.7 %all-to-all-start = ((f32[128,8,256]{2,0,1:T(8,128)}), f32[128,8,256]{2,0,1:T(8,128)S(1)}, u32[]{:S(2)}, u32[]{:S(2)}) async-start(f32[128,8,256]{2,0,1:T(8,128)} %bitcast.24), calls=%async_computation | async-start | bytes 2097152 | tf_op jit(solution)/shard_map/all_to_all | solution.py:18
  25.7 392.4 %all-reduce.3.cloned.1.call-start = ((), (), s32[]{:S(2)}) async-start(), calls=%async_computation.2 | async-start | bytes 524288 | tf_op jit(solution)/shard_map/psum | solution.py:27
  138.2 470.2 %all-reduce.5.cloned.1.call-start = ((), (), s32[]{:S(2)}) async-start(), calls=%async_computation.4 | async-start | bytes 524288 | tf_op jit(solution)/shard_map/psum | solution.py:27
  420.5 1.0 copy-start
Sparse Core Ops, SparseCore 0:
  11.9 119.5 all-gather.2
  133.6 96.2 all-gather.4
  233.4 184.6 all-reduce.2
  424.2 184.1 all-reduce.4
